TPU v7x, 32 devices: a whole 2x2x4 slice. The times are simulated.
32 devices in a mesh: layer: 2 (over x), feat: 4 (over z), tok: 4 (over y, core).
Axes of the slice: x: 2, y: 2, z: 4, core: 2. Of those that a mesh axis runs over, the one named last changes fastest.
Arguments:
- resid: bfloat16 [2, 1024, 2304], P('layer', 'tok', 'feat'), may hold values from -6 to 6
- norm_gain: bfloat16 [2, 2304], P('layer', 'feat'), may hold values from 0.5 to 2
- prev_codes: bfloat16 [1024, 16384], P('tok', 'feat'), may hold values from 0 to 1.5
- feature_mask: int32 [2, 8, 128], P('layer', 'tok', 'feat'), may hold values 0 or 1
- w_gate: bfloat16 [2, 2304, 9216], P('layer', 'tok', 'feat'), may hold values from -0.125 to 0.125
- w_up: bfloat16 [2, 2304, 9216], P('layer', 'tok', 'feat'), may hold values from -0.125 to 0.125
- w_down: bfloat16 [2, 9216, 2304], P('layer', 'feat', 'tok'), may hold values from -0.0625 to 0.0625
- enc_weight: bfloat16 [2, 2304, 16384], P('layer', 'tok', 'feat'), may hold values from -0.125 to 0.125
- enc_bias: float32 [2, 16384], P('layer', 'feat'), may hold values from -3 to 3
- dec_own: bfloat16 [2, 16384, 2304], P('layer', 'feat', 'tok'), may hold values from -0.046875 to 0.046875
- dec_prev: bfloat16 [2, 16384, 2304], P('layer', 'feat', 'tok'), may hold values from -0.046875 to 0.046875
Outputs:
- grad_enc: float32 [2, 2304, 16384], P('layer', 'tok', 'feat')
- grad_bias: float32 [2, 16384], P('layer', 'feat')
- grad_own: float32 [2, 16384, 2304], P('layer', 'feat', 'tok')
- grad_prev: float32 [2, 16384, 2304], P('layer', 'feat', 'tok')
All inputs are finite; a program needn't handle non-finite values. No bound on the sum of `feature_mask` on one device may be relied on, other than what follows from the above.
Results may differ from a plain program's by a relative error of at most 0.0063.
Values may be sent and summed in bfloat16 or wider, within the bound.
A program may use at most 256 MiB of HBM per device.

v0:
```python
import math

import jax
import jax.numpy as jnp
from jax import lax
from jax.sharding import PartitionSpec as P

TILE = 128
TBLK = 128


def passed_along(value, axis, steps):
    count = lax.axis_size(axis)
    leading, last = (max(0, -steps), min(count, count - steps))
    return lax.ppermute(value, axis, [(source, source + steps) for source in range(leading, last)])


def block_keep(block_mask, height, breadth):
    blocks = block_mask.astype(jnp.float32)
    spread = jnp.broadcast_to(
        blocks[:, None, :, None], (blocks.shape[0], TBLK, blocks.shape[1], TILE)
    )
    return spread.reshape(height, breadth)


def local(
    resid,
    norm_gain,
    prev_codes,
    feature_mask,
    w_gate,
    w_up,
    w_down,
    enc_weight,
    enc_bias,
    dec_own,
    dec_prev,
):
    gathered, gains = (
        lax.all_gather(resid[0], "feat", axis=1, tiled=True),
        lax.all_gather(norm_gain, "feat", axis=1, tiled=True),
    )
    stream = gathered.astype(jnp.float32)
    normed = (
        stream
        * lax.rsqrt(jnp.mean(stream * stream, axis=1, keepdims=True) + 1e-06)
        * gains[0].astype(jnp.float32)
    ).astype(jnp.bfloat16)
    height = normed.shape[0]
    feat_local = enc_weight.shape[2]
    segments = (
        lax.all_gather(w_gate[0], "tok", axis=0, tiled=True),
        lax.all_gather(w_up[0], "tok", axis=0, tiled=True),
        lax.all_gather(enc_weight[0], "tok", axis=0, tiled=True),
    )
    gate_sum, up_sum, enc_sum = tuple(
        (jnp.dot(normed, segment, preferred_element_type=jnp.float32) for segment in segments)
    )
    hidden = (jax.nn.gelu(gate_sum, approximate=True) * up_sum).astype(jnp.bfloat16)
    preact = enc_sum + enc_bias[0]
    active = jnp.maximum(preact, 0.0)
    keeper = block_keep(feature_mask[0], height, feat_local)
    codes = (active * active * keeper).astype(jnp.bfloat16)
    shifted = passed_along(codes, "layer", 1)
    source = jnp.where(lax.axis_index("layer") == 0, prev_codes, shifted)
    own_full, prev_full = (
        lax.all_gather(dec_own[0], "tok", axis=1, tiled=True),
        lax.all_gather(dec_prev[0], "tok", axis=1, tiled=True),
    )
    partial_value = (
        jnp.dot(codes, own_full, preferred_element_type=jnp.float32)
        + jnp.dot(source, prev_full, preferred_element_type=jnp.float32)
        - jnp.dot(
            hidden,
            lax.all_gather(w_down[0], "tok", axis=1, tiled=True),
            preferred_element_type=jnp.float32,
        )
    )
    error = lax.psum(partial_value, "feat").astype(jnp.bfloat16)
    own_back = jnp.dot(error, own_full.T, preferred_element_type=jnp.float32)
    prev_back = jnp.dot(error, prev_full.T, preferred_element_type=jnp.float32)
    later = passed_along(prev_back.astype(jnp.bfloat16), "layer", -1).astype(prev_back.dtype)
    back = own_back + later
    factor = 1.0 / math.sqrt(height * lax.axis_size("tok"))
    pregrad = (back * keeper * (2.0 * active) * factor).astype(jnp.bfloat16)
    normed_cols = lax.all_to_all(normed, "tok", split_axis=1, concat_axis=0, tiled=True)
    error_cols = lax.all_to_all(error, "tok", split_axis=1, concat_axis=0, tiled=True)
    codes_all, source_all = (
        lax.all_gather(codes, "tok", axis=0, tiled=True),
        lax.all_gather(source, "tok", axis=0, tiled=True),
    )
    pregrad_all = lax.all_gather(pregrad, "tok", axis=0, tiled=True)
    grad_enc = jnp.dot(normed_cols.T, pregrad_all, preferred_element_type=jnp.float32)
    grad_bias = jnp.sum(pregrad_all.astype(jnp.float32), axis=0)
    grad_own = jnp.dot(codes_all.T, error_cols, preferred_element_type=jnp.float32) * factor
    grad_prev = jnp.dot(source_all.T, error_cols, preferred_element_type=jnp.float32) * factor
    return (grad_enc[None], grad_bias[None], grad_own[None], grad_prev[None])


def solution(mesh):
    in_specs = (
        P("layer", "tok", "feat"),
        P("layer", "feat"),
        P("tok", "feat"),
        P("layer", "tok", "feat"),
        P("layer", "tok", "feat"),
        P("layer", "tok", "feat"),
        P("layer", "feat", "tok"),
        P("layer", "tok", "feat"),
        P("layer", "feat"),
        P("layer", "feat", "tok"),
        P("layer", "feat", "tok"),
    )
    out_specs = (
        P("layer", "tok", "feat"),
        P("layer", "feat"),
        P("layer", "feat", "tok"),
        P("layer", "feat", "tok"),
    )
    return jax.shard_map(local, mesh=mesh, in_specs=in_specs, out_specs=out_specs, check_vma=False)
```

profile of v0, /device:TPU:0, one launch (start us, length us, event | category | flops | bytes accessed | tf_op | source)
XLA Modules:
  0.0 905.5 jit_solution(4202386493531622728)
XLA Ops:
  11.2 0.7 all-gather.36.cloned.1.call-update
  13.5 14.1 %all-reduce = bf16[2304]{0:T(1024)(128)(2,1)S(1)} all-reduce(bf16[2304]{0:T(1024)(128)(2,1)S(1)} %dynamic-update-slice), channel_id=1, replica_groups=mesh['layer'=2,'feat'=4,'tok'=4] {'feat'}, use_global_device_ids=true, to_apply=%add | all-reduce | flops 2304 | bytes 9216
  27.6 15.1 %all-gather.24.cloned.1.call-done = bf16[1,256,2304]{1,2,0:T(8,128)(2,1)} async-done(((bf16[1,256,576]{1,2,0:T(8,128)(2,1)}), bf16[1,256,2304]{1,2,0:T(8,128)(2,1)}) %all-gather.24.cloned.1.call-update) | async-done | bytes 1179664 | tf_op jit(solution)/shard_map/all_gather | solution.py:40
  42.7 1.6 fusion.41
  44.4 2.7 fusion.43
  47.0 116.6 %all-gather.26.cloned.1.call-done = bf16[1,2304,4096]{2,1,0:T(8,128)(2,1)} async-done(((bf16[1,576,4096]{2,1,0:T(8,128)(2,1)}), bf16[1,2304,4096]{2,1,0:T(8,128)(2,1)}) %all-gather.26.cloned.1.call-update) | async-done | bytes 18874384 | tf_op jit(solution)/shard_map/all_gather | solution.py:54
  164.2 16.5 %fusion.25 = (bf16[256,4096]{1,0:T(8,128)(2,1)}, f32[256,4096]{1,0:T(8,128)}) fusion(f32[32,8,32,128]{3,2,1,0:T(8,128)S(1)} %bitcast.93, f32[4096]{0:T(1024)S(1)} %bitcast.100, bf16[256,2304]{0,1:T(8,128)(2,1)} %fusion.43, bf16[1,2304,4096]{2,1,0:T(8,128)(2,1)} %all-gather.26.cloned.1.call-done), kind=kOutput, calls=%fused_computation.25 | convolution fusion | flops 4837081088 | bytes 30556160 | tf_op jit(solution)/shard_map/dot_general | solution.py:57
  180.8 4.7 collective-permute-start
  185.5 50.6 %all-gather.32.cloned.1.call-done = bf16[1,2304,2304]{2,1,0:T(8,128)(2,1)} async-done(((bf16[1,576,2304]{2,1,0:T(8,128)(2,1)}), bf16[1,2304,2304]{2,1,0:T(8,128)(2,1)}) %all-gather.32.cloned.1.call-update) | async-done | bytes 10616848 | tf_op jit(solution)/shard_map/all_gather | solution.py:52
  236.1 9.3 %fusion.50 = f32[256,2304]{1,0:T(8,128)} fusion(bf16[256,2304]{0,1:T(8,128)(2,1)} %fusion.43, bf16[1,2304,2304]{2,1,0:T(8,128)(2,1)} %all-gather.32.cloned.1.call-done), kind=kOutput, calls=%fused_computation.45 | convolution fusion | flops 2722627584 | bytes 14155776 | tf_op jit(solution)/shard_map/dot_general | solution.py:57
  245.4 1.5 broadcast_select_fusion
  247.2 110.3 %all-gather.28.cloned.1.call-done = bf16[1,4096,2304]{1,2,0:T(8,128)(2,1)} async-done(((bf16[1,4096,576]{1,2,0:T(8,128)(2,1)}), bf16[1,4096,2304]{1,2,0:T(8,128)(2,1)}) %all-gather.28.cloned.1.call-update) | async-done | bytes 18874384 | tf_op jit(solution)/shard_map/all_gather | solution.py:67
  357.5 10.4 %fusion.6 = f32[256,2304]{1,0:T(8,128)} fusion(bf16[256,4096]{1,0:T(8,128)(2,1)S(1)} %copy-done.2, bf16[1,4096,2304]{1,2,0:T(8,128)(2,1)} %all-gather.28.cloned.1.call-done), kind=kOutput, calls=%fused_computation.6 | convolution fusion | flops 4831838208 | bytes 23330816 | tf_op jit(solution)/shard_map/dot_general | solution.py:71
  368.0 111.0 %all-gather.30.cloned.1.call-done = bf16[1,4096,2304]{1,2,0:T(8,128)(2,1)} async-done(((bf16[1,4096,576]{1,2,0:T(8,128)(2,1)}), bf16[1,4096,2304]{1,2,0:T(8,128)(2,1)}) %all-gather.30.cloned.1.call-update) | async-done | bytes 18874384 | tf_op jit(solution)/shard_map/all_gather | solution.py:68
  479.0 11.7 %fusion.35 = f32[256,2304]{1,0:T(8,128)} fusion(f32[256,2304]{1,0:T(8,128)} %fusion.6, bf16[256,4096]{1,0:T(8,128)(2,1)} %broadcast_select_fusion, bf16[1,4096,2304]{1,2,0:T(8,128)(2,1)} %all-gather.30.cloned.1.call-done), kind=kOutput, calls=%fused_computation.31 | convolution fusion | flops 4832428032 | bytes 25690112 | tf_op jit(solution)/shard_map/dot_general | solution.py:72
  490.7 60.7 %all-gather.34.cloned.1.call-done = bf16[1,2304,2304]{2,1,0:T(8,128)(2,1)} async-done(((bf16[1,576,2304]{2,1,0:T(8,128)(2,1)}), bf16[1,2304,2304]{2,1,0:T(8,128)(2,1)}) %all-gather.34.cloned.1.call-update) | async-done | bytes 10616848 | tf_op jit(solution)/shard_map/all_gather | solution.py:53
  551.3 72.5 %all-gather.36.cloned.1.call-done = bf16[1,2304,2304]{1,2,0:T(8,128)(2,1)} async-done(((bf16[1,2304,576]{1,2,0:T(8,128)(2,1)}), bf16[1,2304,2304]{1,2,0:T(8,128)(2,1)}) %all-gather.36.cloned.1.call-update) | async-done | bytes 10616848 | tf_op jit(solution)/shard_map/all_gather | solution.py:75
  623.9 15.3 %fusion.32 = f32[256,2304]{1,0:T(8,128)S(1)} fusion(f32[256,2304]{1,0:T(8,128)} %fusion.35, bf16[1,2304,2304]{1,2,0:T(8,128)(2,1)} %all-gather.36.cloned.1.call-done, f32[256,2304]{1,0:T(8,128)} %fusion.50, bf16[256,2304]{0,1:T(8,128)(2,1)} %fusion.43, bf16[1,2304,2304]{2,1,0:T(8,128)(2,1)} %all-gather.34.cloned.1.call-done), kind=kOutput, calls=%fused_computation.30 | convolution fusion | flops 5437587456 | bytes 29491200 | tf_op jit(solution)/shard_map/dot_general | solution.py:73
  639.2 87.3 %all-reduce.2 = bf16[256,2304]{1,0:T(8,128)(2,1)S(1)} all-reduce(f32[256,2304]{1,0:T(8,128)S(1)} %fusion.32), channel_id=1, replica_groups=mesh['layer'=2,'feat'=4,'tok'=4] {'feat'}, use_global_device_ids=true, to_apply=%region_1.2 | all-reduce | flops 589824 | bytes 3538944 | tf_op jit(solution)/shard_map/psum | solution.py:79
  726.5 10.1 %fusion.22 = bf16[256,4096]{1,0:T(8,128)(2,1)S(1)} fusion(bf16[256,2304]{1,0:T(8,128)(2,1)S(1)} %all-reduce.2, bf16[1,4096,2304]{1,2,0:T(8,128)(2,1)} %all-gather.30.cloned.1.call-done), kind=kOutput, calls=%fused_computation.22 | convolution fusion | flops 4832886784 | bytes 22151168 | tf_op jit(solution)/shard_map/dot_general | solution.py:81
  736.6 1.3 collective-permute-start.1
  737.9 46.5 %collective-permute-done.1 = bf16[256,4096]{1,0:T(8,128)(2,1)S(1)} collective-permute-done((bf16[256,4096]{1,0:T(8,128)(2,1)S(1)}, bf16[256,4096]{1,0:T(8,128)(2,1)S(1)}, u32[]{:S(2)}, u32[]{:S(2)}) %collective-permute-start.1) | collective-permute-done | bytes 2097184 | tf_op jit(solution)/shard_map/ppermute | solution.py:15
  784.4 16.2 %fusion.28 = bf16[256,4096]{1,0:T(8,128)(2,1)} fusion(f32[256,4096]{1,0:T(8,128)S(1)} %copy-done.4, bf16[256,4096]{1,0:T(8,128)(2,1)S(1)} %collective-permute-done.1, f32[32,8,32,128]{3,2,1,0:T(8,128)S(1)} %bitcast.94, bf16[256,2304]{1,0:T(8,128)(2,1)S(1)} %all-reduce.2, bf16[1,4096,2304]{1,2,0:T(8,128)(2,1)} %all-gather.28.cloned.1.call-done), kind=kOutput, calls=%fused_computation.28 | convolution fusion | flops 4839178240 | bytes 32636928 | tf_op jit(solution)/shard_map/dot_general | solution.py:80
  800.7 3.5 all-to-all-start
  804.2 1.4 copy.19
  805.7 25.4 %all-to-all-done = bf16[256,4,576]{0,2,1:T(8,128)(2,1)S(1)} async-done(((bf16[256,4,576]{0,2,1:T(8,128)(2,1)}), bf16[256,4,576]{0,2,1:T(8,128)(2,1)S(1)}, u32[]{:S(2)}, u32[]{:S(2)}) %all-to-all-start) | async-done | bytes 1179680 | tf_op jit(solution)/shard_map/all_to_all | solution.py:86
  831.1 3.8 all-to-all-start.1
  835.0 28.4 %all-to-all-done.1 = bf16[256,4,576]{0,2,1:T(8,128)(2,1)S(1)} async-done(((bf16[256,4,576]{0,2,1:T(8,128)(2,1)}), bf16[256,4,576]{0,2,1:T(8,128)(2,1)S(1)}, u32[]{:S(2)}, u32[]{:S(2)}) %all-to-all-start.1) | async-done | bytes 1179680 | tf_op jit(solution)/shard_map/all_to_all | solution.py:87
  863.7 10.9 %multiply_bitcast_fusion.1 = f32[1,4096,576]{1,2,0:T(8,128)} fusion(bf16[1024,576]{0,1:T(8,128)(2,1)S(1)} %bitcast.98, bf16[1024,4096]{1,0:T(8,128)(2,1)} %all-gather.20.cloned.1.call-done), kind=kOutput, calls=%fused_computation.18 | convolution fusion | flops 4834197504 | bytes 19005440 | tf_op jit(solution)/shard_map/dot_general | solution.py:95
  874.5 10.8 %multiply_bitcast_fusion = f32[1,4096,576]{1,2,0:T(8,128)} fusion(bf16[1024,576]{0,1:T(8,128)(2,1)S(1)} %bitcast.99, bf16[1024,4096]{1,0:T(8,128)(2,1)} %all-gather.22.cloned.1.call-done), kind=kOutput, calls=%fused_computation.17 | convolution fusion | flops 4834197504 | bytes 19005440 | tf_op jit(solution)/shard_map/dot_general | solution.py:96
  885.4 5.3 convert_reduce_fusion
  891.1 7.5 convolution_bitcast_fusion
  (53 shorter events, 6.5 us)
Async XLA Ops:
  7.2 35.6 %all-gather.24.cloned.1.call-start = ((), (), s32[]{:S(2)}) async-start(), calls=%async_computation.5 | async-start | bytes 1474560 | tf_op jit(solution)/shard_map/all_gather | solution.py:40
  7.9 155.7 %all-gather.26.cloned.1.call-start = ((), (), s32[]{:S(2)}) async-start(), calls=%async_computation.6 | async-start | bytes 23592960 | tf_op jit(solution)/shard_map/all_gather | solution.py:54
  8.6 227.4 %all-gather.32.cloned.1.call-start = ((), (), s32[]{:S(2)}) async-start(), calls=%async_computation.9 | async-start | bytes 13271040 | tf_op jit(solution)/shard_map/all_gather | solution.py:52
  9.4 348.2 %all-gather.28.cloned.1.call-start = ((), (), s32[]{:S(2)}) async-start(), calls=%async_computation.7 | async-start | bytes 23592960 | tf_op jit(solution)/shard_map/all_gather | solution.py:67
  10.0 469.0 %all-gather.30.cloned.1.call-start = ((), (), s32[]{:S(2)}) async-start(), calls=%async_computation.8 | async-start | bytes 23592960 | tf_op jit(solution)/shard_map/all_gather | solution.py:68
  10.5 1.4 copy-start.9
  10.6 2.7 copy-start.7
  10.6 17.0 %copy-start.8 = (s32[1,2,32]{2,1,0:T(2,128)S(1)}, s32[1,2,32]{2,1,0:T(2,128)}, u32[]{:S(2)}) copy-start(s32[1,2,32]{2,1,0:T(2,128)} %param.14) | copy-start | bytes 772
  10.6 540.8 %all-gather.34.cloned.1.call-start = ((), (), s32[]{:S(2)}) async-start(), calls=%async_computation.10 | async-start | bytes 13271040 | tf_op jit(solution)/shard_map/all_gather | solution.py:53
  11.2 612.7 %all-gather.36.cloned.1.call-start = ((), (), s32[]{:S(2)}) async-start(), calls=%async_computation.11 | async-start | bytes 13271040 | tf_op jit(solution)/shard_map/all_gather | solution.py:75
  11.9 851.7 %all-gather.20.cloned.1.call-start = ((), (), s32[]{:S(2)}) async-start(), calls=%async_computation.3 | async-start | bytes 10485760 | tf_op jit(solution)/shard_map/all_gather | solution.py:89
  47.0 117.2 %copy-start.6 = (f32[1,4096]{1,0:T(1,128)S(1)}, f32[1,4096]{1,0:T(1,128)}, u32[]{:S(2)}) copy-start(f32[1,4096]{1,0:T(1,128)} %param.19) | copy-start | bytes 49156
  164.2 16.5 %copy-start = (f32[2,128,32,128]{3,2,1,0:T(8,128)}, f32[2,128,32,128]{3,2,1,0:T(8,128)S(1)}, u32[]{:S(2)}) copy-start(f32[2,128,32,128]{3,2,1,0:T(8,128)S(1)} %broadcast_in_dim.20) | copy-start | bytes 12582916
  180.7 693.8 %all-gather.22.cloned.1.call-start = ((), (), s32[]{:S(2)}) async-start(), calls=%async_computation.4 | async-start | bytes 10485760 | tf_op jit(solution)/shard_map/all_gather | solution.py:90
  180.8 64.6 %collective-permute-start = (bf16[256,4096]{1,0:T(8,128)(2,1)}, bf16[256,4096]{1,0:T(8,128)(2,1)}, u32[]{:S(2)}, u32[]{:S(2)}) collective-permute-start(bf16[256,4096]{1,0:T(8,128)(2,1)} %get-tuple-element.4), channel_id=1, source_target_pairs={{0,16},{1,17},{2,18},{3,19},{4,20},{5,21},{6,22},{7,23},{8,24},{9,... | collective-permute-start | bytes 6291464 | tf_op jit(solution)/shard_map/ppermute | solution.py:15
  236.1 9.3 %copy-start.5 = (bf16[256,4096]{1,0:T(8,128)(2,1)S(1)}, bf16[256,4096]{1,0:T(8,128)(2,1)}, u32[]{:S(2)}) copy-start(bf16[256,4096]{1,0:T(8,128)(2,1)} %param.13) | copy-start | bytes 6291460
  245.4 112.1 %copy-start.2 = (bf16[256,4096]{1,0:T(8,128)(2,1)S(1)}, bf16[256,4096]{1,0:T(8,128)(2,1)}, u32[]{:S(2)}) copy-start(bf16[256,4096]{1,0:T(8,128)(2,1)} %get-tuple-element.4) | copy-start | bytes 6291460
  247.0 638.4 %all-gather.18.cloned.1.call-start = ((), (), s32[]{:S(2)}) async-start(), calls=%async_computation.2 | async-start | bytes 10485760 | tf_op jit(solution)/shard_map/all_gather | solution.py:92
  726.5 57.9 %copy-start.1 = (f32[2,128,32,128]{3,2,1,0:T(8,128)S(1)}, f32[2,128,32,128]{3,2,1,0:T(8,128)}, u32[]{:S(2)}) copy-start(f32[2,128,32,128]{3,2,1,0:T(8,128)} %copy-done) | copy-start | bytes 12582916
  726.5 57.9 %copy-start.4 = (f32[256,4096]{1,0:T(8,128)S(1)}, f32[256,4096]{1,0:T(8,128)}, u32[]{:S(2)}) copy-start(f32[256,4096]{1,0:T(8,128)} %get-tuple-element.5) | copy-start | bytes 12582916
  736.6 47.8 %collective-permute-start.1 = (bf16[256,4096]{1,0:T(8,128)(2,1)S(1)}, bf16[256,4096]{1,0:T(8,128)(2,1)S(1)}, u32[]{:S(2)}, u32[]{:S(2)}) collective-permute-start(bf16[256,4096]{1,0:T(8,128)(2,1)S(1)} %fusion.22), channel_id=1, source_target_pairs={{16,0},{17,1},{18,2},{19,3},{20,4},{21,5},{22,6},{23,7},{24,8},{25... | collective-permute-start | bytes 6291464 | tf_op jit(solution)/shard_map/ppermute | solution.py:15
  800.7 30.4 %all-to-all-start = ((bf16[256,4,576]{0,2,1:T(8,128)(2,1)}), bf16[256,4,576]{0,2,1:T(8,128)(2,1)S(1)}, u32[]{:S(2)}, u32[]{:S(2)}) async-start(bf16[256,4,576]{0,2,1:T(8,128)(2,1)} %bitcast.3), calls=%async_computation | async-start | bytes 2359296 | tf_op jit(solution)/shard_map/all_to_all | solution.py:86
  831.1 32.4 %all-to-all-start.1 = ((bf16[256,4,576]{0,2,1:T(8,128)(2,1)}), bf16[256,4,576]{0,2,1:T(8,128)(2,1)S(1)}, u32[]{:S(2)}, u32[]{:S(2)}) async-start(bf16[256,4,576]{0,2,1:T(8,128)(2,1)} %bitcast.15), calls=%async_computation.1 | async-start | bytes 2359296 | tf_op jit(solution)/shard_map/all_to_all | solution.py:87
  885.4 5.8 copy-start.3
Sparse Core Ops, SparseCore 0:
  9.5 33.1 all-gather.23
  44.3 119.2 all-gather.25
  165.1 70.9 all-gather.31
  237.5 119.9 all-gather.27
  359.0 119.9 all-gather.29
  480.4 70.9 all-gather.33
  552.9 70.9 all-gather.35
  625.4 58.2 all-gather.19
  685.3 58.2 all-gather.21
  800.8 78.5 all-gather.17
where the time goes:
time: 906 us; the launch traced here: 905 us
  waiting for transfers between devices  642 us (71%)
  matrix products  119 us (13%)
  blocking collectives  101 us (11%)
  between operations  15 us (2%)
  starting transfers between devices  13.9 us (2%)
  other arithmetic  11.2 us (1%)
    all_gather x1, waiting for transfers between devices, local(): lax.all_gather(enc_weight[0], 'tok', axis=0, tiled=True)  117 us
    all_gather x1, waiting for transfers between devices, local(): lax.all_gather(dec_prev[0], 'tok', axis=1, tiled=True)  111 us
    all_gather x1, waiting for transfers between devices, local(): lax.all_gather(dec_own[0], 'tok', axis=1, tiled=True)  110 us
    psum x1, blocking collectives, local(): error = lax.psum(partial_value, 'feat').astype(jnp.bfloat16)  87.3 us
    all_gather x1, waiting for transfers between devices, local(): lax.all_gather(w_down[0], 'tok', axis=1, tiled=True)  72.5 us
    all_gather x1, waiting for transfers between devices, local(): lax.all_gather(w_up[0], 'tok', axis=0, tiled=True)  60.7 us
    all_gather x1, waiting for transfers between devices, local(): lax.all_gather(w_gate[0], 'tok', axis=0, tiled=True)  50.6 us
    ppermute x2, waiting for transfers between devices, passed_along(): lax.ppermute(value, axis, [(source, source + steps) for source in range(l...  46.5 us
  transfers between devices with their start and end apart: 14, of which 10 were waited for; matrix products, arithmetic and copies ran while one was open for 13% of the time, Pallas kernels for 0%

commit v1 on v0

v1 whole, which is shorter than its diff:
```python
import math

import jax
import jax.numpy as jnp
from jax import lax
from jax.sharding import PartitionSpec as P

TILE = 128
TBLK = 128


def passed_along(value, axis, steps):
    count = lax.axis_size(axis)
    leading, last = (max(0, -steps), min(count, count - steps))
    return lax.ppermute(value, axis, [(source, source + steps) for source in range(leading, last)])


def swapped(value, axis, bit):
    return lax.ppermute(value, axis, [(i, i ^ bit) for i in range(lax.axis_size(axis))])


def levels(axis):
    return [1 << k for k in range(lax.axis_size(axis).bit_length() - 1)]


def relative_blocks(axis):
    order = [0]
    for bit in reversed(levels(axis)):
        order += [r ^ bit for r in order]
    return order


def spread_blocks(value, axis):
    for bit in reversed(levels(axis)):
        value = jnp.concatenate([value, swapped(value, axis, bit)], axis=0)
    return value


def summed_block(product, rows, axis):
    first, *others = levels(axis)
    half = rows.shape[0] // 2
    away = product(rows[half:]).astype(jnp.bfloat16)
    total = product(rows[:half]) + swapped(away, axis, first).astype(jnp.float32)
    for bit in others:
        half = total.shape[0] // 2
        away = total[half:].astype(jnp.bfloat16)
        total = total[:half] + swapped(away, axis, bit).astype(jnp.float32)
    return total


def block_keep(block_mask, height, breadth):
    blocks = block_mask.astype(jnp.float32)
    spread = jnp.broadcast_to(
        blocks[:, None, :, None], (blocks.shape[0], TBLK, blocks.shape[1], TILE)
    )
    return spread.reshape(height, breadth)


def local(
    resid,
    norm_gain,
    prev_codes,
    feature_mask,
    w_gate,
    w_up,
    w_down,
    enc_weight,
    enc_bias,
    dec_own,
    dec_prev,
):
    gathered, gains = (
        lax.all_gather(resid[0], "feat", axis=1, tiled=True),
        lax.all_gather(norm_gain, "feat", axis=1, tiled=True),
    )
    stream = gathered.astype(jnp.float32)
    normed = (
        stream
        * lax.rsqrt(jnp.mean(stream * stream, axis=1, keepdims=True) + 1e-06)
        * gains[0].astype(jnp.float32)
    ).astype(jnp.bfloat16)
    height = normed.shape[0]
    width = enc_weight.shape[1]
    feat_local = enc_weight.shape[2]
    here = lax.axis_index("tok")
    pieces = []
    for r in relative_blocks("tok"):
        piece = lax.dynamic_slice_in_dim(normed, (here ^ r) * width, width, axis=1)
        pieces.append(swapped(piece, "tok", r) if r else piece)
    normed_cols = jnp.concatenate(pieces, axis=0)

    def times(weight):
        return lambda rows: jnp.dot(rows, weight, preferred_element_type=jnp.float32)

    enc_sum = summed_block(times(enc_weight[0]), normed_cols, "tok")
    gate_sum = summed_block(times(w_gate[0]), normed_cols, "tok")
    up_sum = summed_block(times(w_up[0]), normed_cols, "tok")
    hidden = (jax.nn.gelu(gate_sum, approximate=True) * up_sum).astype(jnp.bfloat16)
    preact = enc_sum + enc_bias[0]
    active = jnp.maximum(preact, 0.0)
    keeper = block_keep(feature_mask[0], height, feat_local)
    codes = (active * active * keeper).astype(jnp.bfloat16)
    shifted = passed_along(codes, "layer", 1)
    source = jnp.where(lax.axis_index("layer") == 0, prev_codes, shifted)
    codes_all = spread_blocks(codes, "tok")
    hidden_all = spread_blocks(hidden, "tok")
    source_all = spread_blocks(source, "tok")
    partial_value = (
        jnp.dot(codes_all, dec_own[0], preferred_element_type=jnp.float32)
        + jnp.dot(source_all, dec_prev[0], preferred_element_type=jnp.float32)
        - jnp.dot(hidden_all, w_down[0], preferred_element_type=jnp.float32)
    )
    groups = lax.axis_size("feat")
    terms = partial_value.reshape(groups, partial_value.shape[0] // groups, width)
    terms = lax.all_to_all(terms, "feat", split_axis=0, concat_axis=0, tiled=True)
    error_part = jnp.sum(terms, axis=0).astype(jnp.bfloat16)
    error_cols = lax.all_gather(error_part, "feat", axis=0, tiled=True)
    prev_back = summed_block(times(dec_prev[0].T), error_cols, "tok")
    later = passed_along(prev_back.astype(jnp.bfloat16), "layer", -1).astype(prev_back.dtype)
    own_back = summed_block(times(dec_own[0].T), error_cols, "tok")
    back = own_back + later
    factor = 1.0 / math.sqrt(height * lax.axis_size("tok"))
    pregrad = (back * keeper * (2.0 * active) * factor).astype(jnp.bfloat16)
    pregrad_all = spread_blocks(pregrad, "tok")
    grad_own = jnp.dot(codes_all.T, error_cols, preferred_element_type=jnp.float32) * factor
    grad_prev = jnp.dot(source_all.T, error_cols, preferred_element_type=jnp.float32) * factor
    grad_enc = jnp.dot(normed_cols.T, pregrad_all, preferred_element_type=jnp.float32)
    grad_bias = jnp.sum(pregrad_all.astype(jnp.float32), axis=0)
    return (grad_enc[None], grad_bias[None], grad_own[None], grad_prev[None])


def solution(mesh):
    in_specs = (
        P("layer", "tok", "feat"),
        P("layer", "feat"),
        P("tok", "feat"),
        P("layer", "tok", "feat"),
        P("layer", "tok", "feat"),
        P("layer", "tok", "feat"),
        P("layer", "feat", "tok"),
        P("layer", "tok", "feat"),
        P("layer", "feat"),
        P("layer", "feat", "tok"),
        P("layer", "feat", "tok"),
    )
    out_specs = (
        P("layer", "tok", "feat"),
        P("layer", "feat"),
        P("layer", "feat", "tok"),
        P("layer", "feat", "tok"),
    )
    return jax.shard_map(local, mesh=mesh, in_specs=in_specs, out_specs=out_specs, check_vma=False)
```

time: 906 us -> 634 us (0.70)
  waiting for transfers between devices: 642 us -> 385 us
  blocking collectives: 101 us -> 70.8 us
  matrix products: 119 us -> 92 us
  other arithmetic: 11.2 us -> 33.5 us
  starting transfers between devices: 13.9 us -> 23.2 us
    all_gather x9 -> x1, waiting for transfers between devices: 522 us -> 30 us  [local(): error_cols = lax.all_gather(error_part, 'feat', axis=0, tiled=True)]
    ppermute x0 -> x21, waiting for transfers between devices: none -> 295 us  [swapped(): lax.ppermute(value, axis, [(i, i ^ bit) for i in range(lax.axis_size(axis...]
    psum x1 -> x0, blocking collectives: 87.3 us -> none  [local(): error = lax.psum(partial_value, 'feat').astype(jnp.bfloat16)]
    all_to_all x0 -> x1, blocking collectives: none -> 56.9 us  [local(): lax.all_to_all(terms, 'feat', split_axis=0, concat_axis=0, tiled=True)]
    all_to_all x2 -> x0, waiting for transfers between devices: 53.9 us -> none  [the longest x1 28.4 us: local(): lax.all_to_all(error, 'tok', split_axis=1, concat_axis=0, tiled=True)]
    dot_general x7 -> x13, matrix products: 89.6 us -> 65.6 us  [the longest x10 42.9 us: times(): jnp.dot(rows, weight, preferred_element_type=jnp.float32)]
    convert_element_type x0 -> x4, other arithmetic: none -> 17.8 us  [the longest x1 6.5 us: local(): pregrad = (back * keeper * (2.0 * active) * factor).astype(jnp.bfloat16)]
    ppermute x0 -> x21, starting transfers between devices: none -> 16.1 us  [swapped(): lax.ppermute(value, axis, [(i, i ^ bit) for i in range(lax.axis_size(axis...]
  transfers between devices with their start and end apart: 14 -> 25, of which waited for: 10 -> 17; matrix products, arithmetic and copies ran while one was open for 13% -> 14% of each run, Pallas kernels for 0% -> 0%
where the time goes in v1:
time: 634 us; the launch traced here: 626 us
  waiting for transfers between devices  385 us (61%)
  matrix products  92 us (15%)
  blocking collectives  70.8 us (11%)
  other arithmetic  33.5 us (5%)
  starting transfers between devices  23.2 us (4%)
  between operations  15.7 us (2%)
    ppermute x21, waiting for transfers between devices, swapped(): lax.ppermute(value, axis, [(i, i ^ bit) for i in range(lax.axis_size(axis...  295 us
    all_to_all x1, blocking collectives, local(): lax.all_to_all(terms, 'feat', split_axis=0, concat_axis=0, tiled=True)  56.9 us
    dot_general x10, matrix products, times(): jnp.dot(rows, weight, preferred_element_type=jnp.float32)  42.9 us
    ppermute x2, waiting for transfers between devices, passed_along(): lax.ppermute(value, axis, [(source, source + steps) for source in range(l...  40.8 us
    all_gather x1, waiting for transfers between devices, local(): error_cols = lax.all_gather(error_part, 'feat', axis=0, tiled=True)  30 us
    all_gather x1, waiting for transfers between devices, local(): lax.all_gather(resid[0], 'feat', axis=1, tiled=True)  18 us
    ppermute x21, starting transfers between devices, swapped(): lax.ppermute(value, axis, [(i, i ^ bit) for i in range(lax.axis_size(axis...  16.1 us
    unnamed x1, blocking collectives  13.9 us
  transfers between devices with their start and end apart: 25, of which 17 were waited for; matrix products, arithmetic and copies ran while one was open for 14% of the time, Pallas kernels for 0%

profile of v1, /device:TPU:0, one launch (start us, length us, event | category | flops | bytes accessed | tf_op | source)
XLA Modules:
  0.0 625.9 jit_solution(14506811225230050466)
XLA Ops:
  10.8 13.9 %all-reduce = bf16[2304]{0:T(1024)(128)(2,1)S(1)} all-reduce(bf16[2304]{0:T(1024)(128)(2,1)S(1)} %dynamic-update-slice), channel_id=1, replica_groups=mesh['layer'=2,'feat'=4,'tok'=4] {'feat'}, use_global_device_ids=true, to_apply=%add | all-reduce | flops 2304 | bytes 9216
  24.7 18.0 %all-gather.6.cloned.1.call-done = bf16[1,256,2304]{1,2,0:T(8,128)(2,1)} async-done(((bf16[1,256,576]{1,2,0:T(8,128)(2,1)}), bf16[1,256,2304]{1,2,0:T(8,128)(2,1)}) %all-gather.6.cloned.1.call-update) | async-done | bytes 1179664 | tf_op jit(solution)/shard_map/all_gather | solution.py:73
  48.0 7.2 %collective-permute-done.2 = bf16[256,576]{0,1:T(8,128)(2,1)S(1)} collective-permute-done((bf16[256,576]{0,1:T(8,128)(2,1)S(1)}, bf16[256,576]{0,1:T(8,128)(2,1)S(1)}, u32[]{:S(2)}, u32[]{:S(2)}) %collective-permute-start.2) | collective-permute-done | bytes 294944 | tf_op jit(solution)/shard_map/ppermute | solution.py:19
  55.1 3.8 convolution_convert_fusion.2
  60.9 7.5 %collective-permute-done = bf16[256,576]{0,1:T(8,128)(2,1)S(1)} collective-permute-done((bf16[256,576]{0,1:T(8,128)(2,1)S(1)}, bf16[256,576]{0,1:T(8,128)(2,1)S(1)}, u32[]{:S(2)}, u32[]{:S(2)}) %collective-permute-start) | collective-permute-done | bytes 294944 | tf_op jit(solution)/shard_map/ppermute | solution.py:19
  73.9 45.3 %collective-permute-done.4 = bf16[256,4096]{1,0:T(8,128)(2,1)S(1)} collective-permute-done((bf16[256,4096]{1,0:T(8,128)(2,1)S(1)}, bf16[256,4096]{1,0:T(8,128)(2,1)S(1)}, u32[]{:S(2)}, u32[]{:S(2)}) %collective-permute-start.4) | collective-permute-done | bytes 2097184 | tf_op jit(solution)/shard_map/ppermute | solution.py:19
  119.8 5.0 fusion.22
  124.8 5.4 collective-permute-start.7
  138.9 33.3 %collective-permute-done.7 = bf16[256,4096]{1,0:T(8,128)(2,1)} collective-permute-done((bf16[256,4096]{1,0:T(8,128)(2,1)}, bf16[256,4096]{1,0:T(8,128)(2,1)}, u32[]{:S(2)}, u32[]{:S(2)}) %collective-permute-start.7) | collective-permute-done | bytes 2097184 | tf_op jit(solution)/shard_map/ppermute | solution.py:15
  175.5 3.7 convolution_add_fusion.1
  185.4 3.7 convolution_add_fusion
  191.7 35.8 %collective-permute-done.8 = bf16[256,4096]{1,0:T(8,128)(2,1)} collective-permute-done((bf16[256,4096]{1,0:T(8,128)(2,1)S(1)}, bf16[256,4096]{1,0:T(8,128)(2,1)}, u32[]{:S(2)}, u32[]{:S(2)}) %collective-permute-start.8) | collective-permute-done | bytes 2097184 | tf_op jit(solution)/shard_map/ppermute | solution.py:19
  229.8 22.9 %collective-permute-done.11 = bf16[256,2304]{1,0:T(8,128)(2,1)} collective-permute-done((bf16[256,2304]{1,0:T(8,128)(2,1)S(1)}, bf16[256,2304]{1,0:T(8,128)(2,1)}, u32[]{:S(2)}, u32[]{:S(2)}) %collective-permute-start.11) | collective-permute-done | bytes 1179680 | tf_op jit(solution)/shard_map/ppermute | solution.py:19
  252.8 24.8 %collective-permute-done.13 = bf16[256,2304]{1,0:T(8,128)(2,1)} collective-permute-done((bf16[256,2304]{1,0:T(8,128)(2,1)}, bf16[256,2304]{1,0:T(8,128)(2,1)}, u32[]{:S(2)}, u32[]{:S(2)}) %collective-permute-start.13) | collective-permute-done | bytes 1179680 | tf_op jit(solution)/shard_map/ppermute | solution.py:19
  281.9 26.1 %collective-permute-done.14 = bf16[256,2304]{1,0:T(8,128)(2,1)S(1)} collective-permute-done((bf16[256,2304]{1,0:T(8,128)(2,1)S(1)}, bf16[256,2304]{1,0:T(8,128)(2,1)S(1)}, u32[]{:S(2)}, u32[]{:S(2)}) %collective-permute-start.14) | collective-permute-done | bytes 1179680 | tf_op jit(solution)/shard_map/ppermute | solution.py:19
  309.6 10.6 %fusion.16 = f32[1024,576]{0,1:T(8,128)} fusion(bf16[1,4096,576]{1,2,0:T(8,128)(2,1)S(1)} %bitcast.85, bf16[512,4096]{1,0:T(8,128)(2,1)} %collective-permute-done.6, bf16[256,4096]{1,0:T(8,128)(2,1)} %collective-permute-done.5, bf16[256,4096]{1,0:T(8,128)(2,1)} %fusion.22), kind=kOutput, calls=%fused_computation.29 | convolution fusion | flops 4857004032 | bytes 15466496 | tf_op jit(solution)/shard_map/dot_general | solution.py:109
  320.3 7.8 %fusion.9 = f32[1024,576]{0,1:T(8,128)S(1)} fusion(bf16[1,4096,576]{1,2,0:T(8,128)(2,1)S(1)} %bitcast.81, bf16[512,4096]{1,0:T(8,128)(2,1)} %collective-permute-done.9, bf16[256,4096]{1,0:T(8,128)(2,1)} %collective-permute-done.8, bf16[256,4096]{1,0:T(8,128)(2,1)S(1)} %broadcast_select_fusion), kind=kOutput, calls=%fused_computation.24 | convolution fusion | flops 4857004032 | bytes 15466496 | tf_op jit(solution)/shard_map/dot_general | solution.py:110
  328.1 4.2 add_subtract_fusion
  332.5 56.9 %all_to_all.5 = f32[4,256,576]{1,2,0:T(8,128)S(1)} all-to-all(f32[4,256,576]{1,2,0:T(8,128)S(1)} %bitcast.79), channel_id=1, replica_groups=mesh['layer'=2,'feat'=4,'tok'=4] {'feat'}, dimensions={0} | all-to-all | bytes 4718592 | tf_op jit(solution)/shard_map/all_to_all | solution.py:115
  390.4 30.0 %all-gather.4.cloned.1.call-done = bf16[1024,576]{0,1:T(8,128)(2,1)} async-done(((bf16[256,576]{0,1:T(8,128)(2,1)}), bf16[1024,576]{0,1:T(8,128)(2,1)}) %all-gather.4.cloned.1.call-update) | async-done | bytes 1179664 | tf_op jit(solution)/shard_map/all_gather | solution.py:117
  420.4 6.1 convolution_convert_fusion
  426.6 6.1 convolution_convert_fusion.1
  433.8 3.6 convert_add_fusion
  440.0 5.4 convert_add_fusion.1
  448.2 38.2 %collective-permute-done.19 = bf16[256,4096]{1,0:T(8,128)(2,1)} collective-permute-done((bf16[256,4096]{1,0:T(8,128)(2,1)S(1)}, bf16[256,4096]{1,0:T(8,128)(2,1)}, u32[]{:S(2)}, u32[]{:S(2)}) %collective-permute-start.19) | collective-permute-done | bytes 2097184 | tf_op jit(solution)/shard_map/ppermute | solution.py:19
  491.4 39.0 %collective-permute-done.17 = bf16[256,4096]{1,0:T(8,128)(2,1)} collective-permute-done((bf16[256,4096]{1,0:T(8,128)(2,1)}, bf16[256,4096]{1,0:T(8,128)(2,1)}, u32[]{:S(2)}, u32[]{:S(2)}) %collective-permute-start.17) | collective-permute-done | bytes 2097184 | tf_op jit(solution)/shard_map/ppermute | solution.py:19
  530.5 7.5 %collective-permute-done.20 = bf16[256,4096]{1,0:T(8,128)(2,1)S(1)} collective-permute-done((bf16[256,4096]{1,0:T(8,128)(2,1)}, bf16[256,4096]{1,0:T(8,128)(2,1)S(1)}, u32[]{:S(2)}, u32[]{:S(2)}) %collective-permute-start.20) | collective-permute-done | bytes 2097184 | tf_op jit(solution)/shard_map/ppermute | solution.py:15
  538.0 6.5 %fusion.25 = bf16[256,4096]{1,0:T(8,128)(2,1)S(1)} fusion(f32[512,4096]{1,0:T(8,128)S(1)} %convert_add_fusion.1, bf16[256,4096]{1,0:T(8,128)(2,1)S(1)} %collective-permute-done.20, bf16[256,4096]{1,0:T(8,128)(2,1)} %collective-permute-done.17, f32[32,8,32,128]{3,2,1,0:T(8,128)S(1)} %bitcast.78, bf16[256,4096]{1,0:T(8,128)(2,1)S(1)} %copy-done.6, ...), kind=kLoop, calls=%fused_computation.40 | loop fusion | flops 13631488 | bytes 20987904 | tf_op jit(solution)/shard_map/convert_element_type | solution.py:123
  545.6 44.1 %collective-permute-done.21 = bf16[256,4096]{1,0:T(8,128)(2,1)S(1)} collective-permute-done((bf16[256,4096]{1,0:T(8,128)(2,1)S(1)}, bf16[256,4096]{1,0:T(8,128)(2,1)S(1)}, u32[]{:S(2)}, u32[]{:S(2)}) %collective-permute-start.21) | collective-permute-done | bytes 2097184 | tf_op jit(solution)/shard_map/ppermute | solution.py:19
  590.1 9.3 %multiply_bitcast_fusion = f32[1,4096,576]{1,2,0:T(8,128)} fusion(bf16[1024,576]{0,1:T(8,128)(2,1)S(1)} %copy-done.12, bf16[512,4096]{1,0:T(8,128)(2,1)} %collective-permute-done.9, bf16[256,4096]{1,0:T(8,128)(2,1)} %collective-permute-done.8, bf16[256,4096]{1,0:T(8,128)(2,1)S(1)} %copy-done.8), kind=kOutput, calls=%fused_computation.1 | convolution fusion | flops 4859363328 | bytes 19005440 | tf_op jit(solution)/shard_map/dot_general | solution.py:126
  599.4 9.6 %multiply_bitcast_fusion.1 = f32[1,4096,576]{1,2,0:T(8,128)} fusion(bf16[1024,576]{0,1:T(8,128)(2,1)S(1)} %copy-done.12, bf16[512,4096]{1,0:T(8,128)(2,1)} %collective-permute-done.6, bf16[256,4096]{1,0:T(8,128)(2,1)} %collective-permute-done.5, bf16[256,4096]{1,0:T(8,128)(2,1)} %fusion.22), kind=kOutput, calls=%fused_computation.2 | convolution fusion | flops 4859363328 | bytes 19005440 | tf_op jit(solution)/shard_map/dot_general | solution.py:125
  611.1 7.5 %convolution_bitcast_fusion = f32[1,576,4096]{2,1,0:T(8,128)} fusion(bf16[512,4096]{1,0:T(8,128)(2,1)S(1)} %collective-permute-done.22, bf16[256,4096]{1,0:T(8,128)(2,1)S(1)} %collective-permute-done.21, bf16[256,4096]{1,0:T(8,128)(2,1)S(1)} %fusion.25, bf16[256,576]{0,1:T(8,128)(2,1)S(1)} %copy-done.14, bf16[256,576]{0,1:T(8,128)(2,1)S(1)} %collective-permute-done.1, ...), kind=kOutput, calls=%fused_computation.9 | convolution fusion | flops 4861722624 | bytes 19005440 | tf_op jit(solution)/shard_map/dot_general | solution.py:127
  (126 shorter events, 61.3 us)
Async XLA Ops:
  7.2 123.0 %copy-start = (bf16[1,576,2304]{2,1,0:T(8,128)(2,1)S(1)}, bf16[1,576,2304]{2,1,0:T(8,128)(2,1)}, u32[]{:S(2)}) copy-start(bf16[1,576,2304]{2,1,0:T(8,128)(2,1)} %param.15) | copy-start | bytes 7962628
  7.2 35.6 %all-gather.6.cloned.1.call-start = ((), (), s32[]{:S(2)}) async-start(), calls=%async_computation.2 | async-start | bytes 1474560 | tf_op jit(solution)/shard_map/all_gather | solution.py:73
  7.9 412.5 %all-gather.4.cloned.1.call-start = ((), (), s32[]{:S(2)}) async-start(), calls=%async_computation.1 | async-start | bytes 1474560 | tf_op jit(solution)/shard_map/all_gather | solution.py:117
  46.3 1.7 collective-permute-start.1
  46.4 8.8 %collective-permute-start.2 = (bf16[256,576]{0,1:T(8,128)(2,1)S(1)}, bf16[256,576]{0,1:T(8,128)(2,1)S(1)}, u32[]{:S(2)}, u32[]{:S(2)}) collective-permute-start(bf16[256,576]{0,1:T(8,128)(2,1)S(1)} %get-tuple-element.5), channel_id=1, source_target_pairs={{0,3},{1,2},{2,1},{3,0},{4,7},{5,6},{6,5},{7,4},{8,11},{9,10},{10,... | collective-permute-start | bytes 884744 | tf_op jit(solution)/shard_map/ppermute | solution.py:19
  58.9 9.5 %collective-permute-start.3 = (bf16[512,4096]{1,0:T(8,128)(2,1)S(1)}, bf16[512,4096]{1,0:T(8,128)(2,1)S(1)}, u32[]{:S(2)}, u32[]{:S(2)}) collective-permute-start(bf16[512,4096]{1,0:T(8,128)(2,1)S(1)} %convolution_convert_fusion.2), channel_id=1, source_target_pairs={{0,1},{1,0},{2,3},{3,2},{4,5},{5,4},{6,7},{7,6},{8,9},{9,8},{10,11... | collective-permute-start | bytes 12582920 | tf_op jit(solution)/shard_map/ppermute | solution.py:19
  59.4 9.0 %collective-permute-start = (bf16[256,576]{0,1:T(8,128)(2,1)S(1)}, bf16[256,576]{0,1:T(8,128)(2,1)S(1)}, u32[]{:S(2)}, u32[]{:S(2)}) collective-permute-start(bf16[256,576]{0,1:T(8,128)(2,1)S(1)} %get-tuple-element.7), channel_id=1, source_target_pairs={{0,2},{1,3},{2,0},{3,1},{4,6},{5,7},{6,4},{7,5},{8,10},{9,11},{10,... | collective-permute-start | bytes 884744 | tf_op jit(solution)/shard_map/ppermute | solution.py:19
  72.3 46.8 %collective-permute-start.4 = (bf16[256,4096]{1,0:T(8,128)(2,1)S(1)}, bf16[256,4096]{1,0:T(8,128)(2,1)S(1)}, u32[]{:S(2)}, u32[]{:S(2)}) collective-permute-start(bf16[256,4096]{1,0:T(8,128)(2,1)S(1)} %slice.113), channel_id=1, source_target_pairs={{0,2},{1,3},{2,0},{3,1},{4,6},{5,7},{6,4},{7,5},{8,10},{9,11},{10,... | collective-permute-start | bytes 6291464 | tf_op jit(solution)/shard_map/ppermute | solution.py:19
  124.8 47.4 %collective-permute-start.7 = (bf16[256,4096]{1,0:T(8,128)(2,1)}, bf16[256,4096]{1,0:T(8,128)(2,1)}, u32[]{:S(2)}, u32[]{:S(2)}) collective-permute-start(bf16[256,4096]{1,0:T(8,128)(2,1)} %fusion.22), channel_id=1, source_target_pairs={{0,16},{1,17},{2,18},{3,19},{4,20},{5,21},{6,22},{7,23},{8,24},{9,... | collective-permute-start | bytes 6291464 | tf_op jit(solution)/shard_map/ppermute | solution.py:15
  133.7 41.8 %collective-permute-start.10 = (bf16[512,2304]{1,0:T(8,128)(2,1)}, bf16[512,2304]{1,0:T(8,128)(2,1)}, u32[]{:S(2)}, u32[]{:S(2)}) collective-permute-start(bf16[512,2304]{1,0:T(8,128)(2,1)} %convolution_convert_fusion.4), channel_id=1, source_target_pairs={{0,1},{1,0},{2,3},{3,2},{4,5},{5,4},{6,7},{7,6},{8,9},{9,8},{10,11... | collective-permute-start | bytes 7077896 | tf_op jit(solution)/shard_map/ppermute | solution.py:19
  133.7 48.8 %collective-permute-start.5 = (bf16[256,4096]{1,0:T(8,128)(2,1)}, bf16[256,4096]{1,0:T(8,128)(2,1)}, u32[]{:S(2)}, u32[]{:S(2)}) collective-permute-start(bf16[256,4096]{1,0:T(8,128)(2,1)} %fusion.22), channel_id=1, source_target_pairs={{0,2},{1,3},{2,0},{3,1},{4,6},{5,7},{6,4},{7,5},{8,10},{9,11},{10,... | collective-permute-start | bytes 6291464 | tf_op jit(solution)/shard_map/ppermute | solution.py:19
  138.6 46.7 %collective-permute-start.12 = (bf16[512,2304]{1,0:T(8,128)(2,1)}, bf16[512,2304]{1,0:T(8,128)(2,1)}, u32[]{:S(2)}, u32[]{:S(2)}) collective-permute-start(bf16[512,2304]{1,0:T(8,128)(2,1)} %convolution_convert_fusion.3), channel_id=1, source_target_pairs={{0,1},{1,0},{2,3},{3,2},{4,5},{5,4},{6,7},{7,6},{8,9},{9,8},{10,11... | collective-permute-start | bytes 7077896 | tf_op jit(solution)/shard_map/ppermute | solution.py:19
  174.0 146.2 %copy-start.7 = (bf16[256,4096]{1,0:T(8,128)(2,1)}, bf16[256,4096]{1,0:T(8,128)(2,1)S(1)}, u32[]{:S(2)}) copy-start(bf16[256,4096]{1,0:T(8,128)(2,1)S(1)} %broadcast_select_fusion) | copy-start | bytes 6291460
  174.0 53.5 %collective-permute-start.8 = (bf16[256,4096]{1,0:T(8,128)(2,1)S(1)}, bf16[256,4096]{1,0:T(8,128)(2,1)}, u32[]{:S(2)}, u32[]{:S(2)}) collective-permute-start(bf16[256,4096]{1,0:T(8,128)(2,1)S(1)} %broadcast_select_fusion), channel_id=1, source_target_pairs={{0,2},{1,3},{2,0},{3,1},{4,6},{5,7},{6,4},{7,5},{8,10},{9,11},{10,... | collective-permute-start | bytes 6291464 | tf_op jit(solution)/shard_map/ppermute | solution.py:19
  179.4 73.4 %collective-permute-start.11 = (bf16[256,2304]{1,0:T(8,128)(2,1)S(1)}, bf16[256,2304]{1,0:T(8,128)(2,1)}, u32[]{:S(2)}, u32[]{:S(2)}) collective-permute-start(bf16[256,2304]{1,0:T(8,128)(2,1)S(1)} %slice.115), channel_id=1, source_target_pairs={{0,2},{1,3},{2,0},{3,1},{4,6},{5,7},{6,4},{7,5},{8,10},{9,11},{10,... | collective-permute-start | bytes 3538952 | tf_op jit(solution)/shard_map/ppermute | solution.py:19
  185.3 124.3 %collective-permute-start.6 = (bf16[512,4096]{1,0:T(8,128)(2,1)S(1)}, bf16[512,4096]{1,0:T(8,128)(2,1)}, u32[]{:S(2)}, u32[]{:S(2)}) collective-permute-start(bf16[512,4096]{1,0:T(8,128)(2,1)S(1)} %pad_maximum_fusion.3), channel_id=1, source_target_pairs={{0,1},{1,0},{2,3},{3,2},{4,5},{5,4},{6,7},{7,6},{8,9},{9,8},{10,11... | collective-permute-start | bytes 12582920 | tf_op jit(solution)/shard_map/ppermute | solution.py:19
  190.2 87.4 %collective-permute-start.13 = (bf16[256,2304]{1,0:T(8,128)(2,1)}, bf16[256,2304]{1,0:T(8,128)(2,1)}, u32[]{:S(2)}, u32[]{:S(2)}) collective-permute-start(bf16[256,2304]{1,0:T(8,128)(2,1)} %slice.114), channel_id=1, source_target_pairs={{0,2},{1,3},{2,0},{3,1},{4,6},{5,7},{6,4},{7,5},{8,10},{9,11},{10,... | collective-permute-start | bytes 3538952 | tf_op jit(solution)/shard_map/ppermute | solution.py:19
  227.5 82.0 %slice-start.6 = ((s8[4718592]{0:T(1024)(128)(4,1)}), s8[4194304]{0:T(1024)(128)(4,1)S(1)}, s32[]{:S(2)}) async-start(s8[4718592]{0:T(1024)(128)(4,1)} %bitcast.84), calls=%async_computation.9 | async-start | bytes 8388608
  229.8 90.5 %collective-permute-start.9 = (bf16[512,4096]{1,0:T(8,128)(2,1)S(1)}, bf16[512,4096]{1,0:T(8,128)(2,1)}, u32[]{:S(2)}, u32[]{:S(2)}) collective-permute-start(bf16[512,4096]{1,0:T(8,128)(2,1)S(1)} %pad_maximum_fusion.4), channel_id=1, source_target_pairs={{0,1},{1,0},{2,3},{3,2},{4,5},{5,4},{6,7},{7,6},{8,9},{9,8},{10,11... | collective-permute-start | bytes 12582920 | tf_op jit(solution)/shard_map/ppermute | solution.py:19
  280.3 27.6 %collective-permute-start.14 = (bf16[256,2304]{1,0:T(8,128)(2,1)S(1)}, bf16[256,2304]{1,0:T(8,128)(2,1)S(1)}, u32[]{:S(2)}, u32[]{:S(2)}) collective-permute-start(bf16[256,2304]{1,0:T(8,128)(2,1)S(1)} %fusion.46), channel_id=1, source_target_pairs={{0,2},{1,3},{2,0},{3,1},{4,6},{5,7},{6,4},{7,5},{8,10},{9,11},{10,... | collective-permute-start | bytes 3538952 | tf_op jit(solution)/shard_map/ppermute | solution.py:19
  309.5 18.6 %collective-permute-start.15 = (bf16[512,2304]{1,0:T(8,128)(2,1)}, bf16[512,2304]{1,0:T(8,128)(2,1)}, u32[]{:S(2)}, u32[]{:S(2)}) collective-permute-start(bf16[512,2304]{1,0:T(8,128)(2,1)} %pad_maximum_fusion.11), channel_id=1, source_target_pairs={{0,1},{1,0},{2,3},{3,2},{4,5},{5,4},{6,7},{7,6},{8,9},{9,8},{10,11... | collective-permute-start | bytes 7077896 | tf_op jit(solution)/shard_map/ppermute | solution.py:19
  426.5 7.2 %collective-permute-start.18 = (bf16[512,4096]{1,0:T(8,128)(2,1)S(1)}, bf16[512,4096]{1,0:T(8,128)(2,1)S(1)}, u32[]{:S(2)}, u32[]{:S(2)}) collective-permute-start(bf16[512,4096]{1,0:T(8,128)(2,1)S(1)} %convolution_convert_fusion), channel_id=1, source_target_pairs={{0,1},{1,0},{2,3},{3,2},{4,5},{5,4},{6,7},{7,6},{8,9},{9,8},{10,11... | collective-permute-start | bytes 12582920 | tf_op jit(solution)/shard_map/ppermute | solution.py:19
  432.7 7.3 %collective-permute-start.16 = (bf16[512,4096]{1,0:T(8,128)(2,1)S(1)}, bf16[512,4096]{1,0:T(8,128)(2,1)S(1)}, u32[]{:S(2)}, u32[]{:S(2)}) collective-permute-start(bf16[512,4096]{1,0:T(8,128)(2,1)S(1)} %convolution_convert_fusion.1), channel_id=1, source_target_pairs={{0,1},{1,0},{2,3},{3,2},{4,5},{5,4},{6,7},{7,6},{8,9},{9,8},{10,11... | collective-permute-start | bytes 12582920 | tf_op jit(solution)/shard_map/ppermute | solution.py:19
  437.4 100.6 %slice-start = ((s8[8388608]{0:T(1024)(128)(4,1)}), s8[4194304]{0:T(1024)(128)(4,1)S(1)}, s32[]{:S(2)}) async-start(s8[8388608]{0:T(1024)(128)(4,1)} %bitcast.75), calls=%async_computation.3 | async-start | bytes 8388608
  437.7 100.3 %slice-start.1 = ((s8[8388608]{0:T(1024)(128)(4,1)}), s8[4194304]{0:T(1024)(128)(4,1)S(1)}, s32[]{:S(2)}) async-start(s8[8388608]{0:T(1024)(128)(4,1)} %bitcast.75), calls=%async_computation.4 | async-start | bytes 8388608
  437.7 48.7 %collective-permute-start.19 = (bf16[256,4096]{1,0:T(8,128)(2,1)S(1)}, bf16[256,4096]{1,0:T(8,128)(2,1)}, u32[]{:S(2)}, u32[]{:S(2)}) collective-permute-start(bf16[256,4096]{1,0:T(8,128)(2,1)S(1)} %slice.111), channel_id=1, source_target_pairs={{0,2},{1,3},{2,0},{3,1},{4,6},{5,7},{6,4},{7,5},{8,10},{9,11},{10,... | collective-permute-start | bytes 6291464 | tf_op jit(solution)/shard_map/ppermute | solution.py:19
  447.1 90.9 %copy-start.4 = (f32[2,128,32,128]{3,2,1,0:T(8,128)S(1)}, f32[2,128,32,128]{3,2,1,0:T(8,128)}, u32[]{:S(2)}) copy-start(f32[2,128,32,128]{3,2,1,0:T(8,128)} %copy-done.3) | copy-start | bytes 12582916
  447.1 90.9 %copy-start.6 = (bf16[256,4096]{1,0:T(8,128)(2,1)S(1)}, bf16[256,4096]{1,0:T(8,128)(2,1)}, u32[]{:S(2)}) copy-start(bf16[256,4096]{1,0:T(8,128)(2,1)} %copy-done.5) | copy-start | bytes 6291460
  447.1 83.3 %collective-permute-start.17 = (bf16[256,4096]{1,0:T(8,128)(2,1)}, bf16[256,4096]{1,0:T(8,128)(2,1)}, u32[]{:S(2)}, u32[]{:S(2)}) collective-permute-start(bf16[256,4096]{1,0:T(8,128)(2,1)} %slice.112), channel_id=1, source_target_pairs={{0,2},{1,3},{2,0},{3,1},{4,6},{5,7},{6,4},{7,5},{8,10},{9,11},{10,... | collective-permute-start | bytes 6291464 | tf_op jit(solution)/shard_map/ppermute | solution.py:19
  489.9 48.1 %collective-permute-start.20 = (bf16[256,4096]{1,0:T(8,128)(2,1)}, bf16[256,4096]{1,0:T(8,128)(2,1)S(1)}, u32[]{:S(2)}, u32[]{:S(2)}) collective-permute-start(bf16[256,4096]{1,0:T(8,128)(2,1)} %fusion.26), channel_id=1, source_target_pairs={{16,0},{17,1},{18,2},{19,3},{20,4},{21,5},{22,6},{23,7},{24,8},{25... | collective-permute-start | bytes 6291464 | tf_op jit(solution)/shard_map/ppermute | solution.py:15
  544.5 45.2 %collective-permute-start.21 = (bf16[256,4096]{1,0:T(8,128)(2,1)S(1)}, bf16[256,4096]{1,0:T(8,128)(2,1)S(1)}, u32[]{:S(2)}, u32[]{:S(2)}) collective-permute-start(bf16[256,4096]{1,0:T(8,128)(2,1)S(1)} %fusion.25), channel_id=1, source_target_pairs={{0,2},{1,3},{2,0},{3,1},{4,6},{5,7},{6,4},{7,5},{8,10},{9,11},{10,... | collective-permute-start | bytes 6291464 | tf_op jit(solution)/shard_map/ppermute | solution.py:19
  590.0 19.0 %collective-permute-start.22 = (bf16[512,4096]{1,0:T(8,128)(2,1)S(1)}, bf16[512,4096]{1,0:T(8,128)(2,1)S(1)}, u32[]{:S(2)}, u32[]{:S(2)}) collective-permute-start(bf16[512,4096]{1,0:T(8,128)(2,1)S(1)} %pad_maximum_fusion.5), channel_id=1, source_target_pairs={{0,1},{1,0},{2,3},{3,2},{4,5},{5,4},{6,7},{7,6},{8,9},{9,8},{10,11... | collective-permute-start | bytes 12582920 | tf_op jit(solution)/shard_map/ppermute | solution.py:19
  (20 other events, 341.3 us)
Sparse Core Ops, SparseCore 0:
  9.6 33.1 all-gather.5
  390.5 29.8 all-gather.3
